TPU v7x, 256 devices: a whole 4x4x8 slice. The times are simulated.
256 devices in a mesh: rep: 16 (over z_lo, x), tp: 16 (over y, z_hi, core).
Axes of the slice: x: 4, y: 4, z: 8 (z_hi: 2, z_lo: 4; z = z_hi * 4 + z_lo), core: 2. Of those that a mesh axis runs over, the one named last changes fastest.
Arguments:
- queries: bfloat16 [16, 512, 4096], P('rep', None, 'tp'), may hold values from -120 to 120
- keys: bfloat16 [16, 512, 4096], P('rep', None, 'tp'), may hold values from -6 to 6
- values: bfloat16 [16, 512, 4096], P('rep', None, 'tp'), may hold values from -6 to 6
- out_weight: bfloat16 [16, 4096, 7168], P('rep', 'tp'), may hold values from -0.09375 to 0.09375
- cotangent: bfloat16 [16, 512, 7168], P('rep', 'tp'), may hold values from -6 to 6
- local_params: bfloat16 [16, 2, 128, 7168], P('rep', None, 'tp'), may hold values from -6 to 6
- global_params: float32 [2, 128, 7168], P(None, 'tp'), may hold values from -6 to 6
- momentum: float32 [2, 128, 7168], P(None, 'tp'), may hold values from -3 to 3
- frag_index: int32 [1], replicated, may hold values from 0 to 1
Outputs:
- branch_out: bfloat16 [16, 512, 7168], P('rep', 'tp')
- weight_grad: bfloat16 [16, 4096, 7168], P('rep', 'tp')
- query_grad: bfloat16 [16, 512, 4096], P('rep', None, 'tp')
- key_grad: bfloat16 [16, 512, 4096], P('rep', None, 'tp')
- value_grad: bfloat16 [16, 512, 4096], P('rep', None, 'tp')
- new_global: float32 [128, 7168], P('tp')
- new_momentum: float32 [128, 7168], P('tp')
All inputs are finite; a program needn't handle non-finite values.
Results may differ from a plain program's by a relative error of at most 0.017.
Values may be sent and summed in bfloat16 or wider, within the bound.
No kernel may reach another device: no remote copies, remote signals or barrier semaphores. Data moves between devices by JAX's collectives and lax.ppermute only.
A program may use at most 128 MiB of HBM per device.

v0:
```python
import jax
import jax.numpy as jnp
from jax import lax
from jax.sharding import PartitionSpec as P

HD = 128
LEN = 512
SEQS = 1
outer_momentum = 0.9
outer_rate = 0.7


def nesterov(outer_old, moment_old, summed):
    average = summed / lax.axis_size("rep")
    pseudo_grad = outer_old - average
    new_momentum = outer_momentum * moment_old + pseudo_grad
    new_global = outer_old - outer_rate * (outer_momentum * new_momentum + pseudo_grad)
    return (new_global, new_momentum)


def outer_update(local_params, global_params, momentum, frag_index):
    chosen = frag_index[0]
    local_sel = lax.dynamic_index_in_dim(local_params[0], chosen, 0, keepdims=False).astype(
        jnp.float32
    )
    outer_old = lax.dynamic_index_in_dim(global_params, chosen, 0, keepdims=False)
    moment_old = lax.dynamic_index_in_dim(momentum, chosen, 0, keepdims=False)
    summed = lax.psum(local_sel.astype(jnp.bfloat16), "rep").astype(jnp.float32)
    return nesterov(outer_old, moment_old, summed)


def inner_step(queries, keys, values, out_weight, cotangent):
    scale = HD ** (-0.5)
    head_cols = queries.shape[2]
    heads_here = head_cols // HD
    tokens = queries.shape[1]
    weight_here = out_weight[0]
    query_heads = queries[0].reshape(SEQS, LEN, heads_here, HD)
    key_heads = keys[0].reshape(SEQS, LEN, heads_here, HD)
    value_heads = values[0].reshape(SEQS, LEN, heads_here, HD)
    scores = (
        jnp.einsum("slhd,smhd->shlm", query_heads, key_heads, preferred_element_type=jnp.float32)
        * scale
    )
    causal = jnp.arange(LEN)[:, None] >= jnp.arange(LEN)[None, :]
    scores = jnp.where(causal[None, None], scores, -1e30)
    top = jnp.max(scores, axis=-1, keepdims=True)
    weights = jnp.exp(scores - top)
    probs = weights / jnp.sum(weights, axis=-1, keepdims=True)
    probs_half = probs.astype(jnp.bfloat16)
    context = jnp.einsum(
        "shlm,smhd->slhd", probs_half, value_heads, preferred_element_type=jnp.float32
    )
    context = context.astype(jnp.bfloat16).reshape(tokens, head_cols)
    context_rows = context
    branch_out = lax.psum_scatter(
        jnp.dot(context_rows, weight_here, preferred_element_type=jnp.float32).astype(jnp.bfloat16),
        "tp",
        scatter_dimension=0,
        tiled=True,
    )
    block_rows = lax.all_gather(cotangent[0], "tp", axis=0, tiled=True)
    part_grad = lax.dot_general(
        block_rows, weight_here, (((1,), (1,)), ((), ())), preferred_element_type=jnp.float32
    )
    context_acc = part_grad
    context_rows = context
    weight_acc = lax.dot_general(
        context_rows, block_rows, (((0,), (0,)), ((), ())), preferred_element_type=jnp.float32
    )
    context_acc, weight_acc = (context_acc, weight_acc)
    weight_grad = weight_acc.astype(jnp.bfloat16)
    context_grad = context_acc.astype(jnp.bfloat16).reshape(SEQS, LEN, heads_here, HD)
    probs_grad = jnp.einsum(
        "slhd,smhd->shlm", context_grad, value_heads, preferred_element_type=jnp.float32
    )
    inner = jnp.sum(probs * probs_grad, axis=-1, keepdims=True)
    score_grad = (probs * (probs_grad - inner) * scale).astype(jnp.bfloat16)
    query_grad = jnp.einsum(
        "shlm,smhd->slhd", score_grad, key_heads, preferred_element_type=jnp.float32
    )
    key_grad = jnp.einsum(
        "shlm,slhd->smhd", score_grad, query_heads, preferred_element_type=jnp.float32
    )
    value_grad = jnp.einsum(
        "shlm,slhd->smhd", probs_half, context_grad, preferred_element_type=jnp.float32
    )
    shaped = [
        g.astype(jnp.bfloat16).reshape(1, tokens, head_cols)
        for g in (query_grad, key_grad, value_grad)
    ]
    return (branch_out[None], weight_grad[None], shaped[0], shaped[1], shaped[2])


def shards(
    queries, keys, values, out_weight, cotangent, local_params, global_params, momentum, frag_index
):
    results = inner_step(queries, keys, values, out_weight, cotangent)
    new_global, new_momentum = outer_update(local_params, global_params, momentum, frag_index)
    return (results[0], results[1], results[2], results[3], results[4], new_global, new_momentum)


def solution(mesh):
    placed = (
        P("rep", None, "tp"),
        P("rep", None, "tp"),
        P("rep", None, "tp"),
        P("rep", "tp", None),
        P("rep", "tp", None),
        P("rep", None, "tp", None),
        P(None, "tp", None),
        P(None, "tp", None),
        P(),
    )
    return jax.shard_map(
        shards,
        mesh=mesh,
        in_specs=placed,
        out_specs=(
            P("rep", "tp", None),
            P("rep", "tp", None),
            P("rep", None, "tp"),
            P("rep", None, "tp"),
            P("rep", None, "tp"),
            P("tp", None),
            P("tp", None),
        ),
        check_vma=False,
    )
```

profile of v0, /device:TPU:128, one launch (start us, length us, event | category | flops | bytes accessed | tf_op | source)
XLA Modules:
  0.0 294.4 jit_solution(1788196400667213289)
XLA Ops:
  8.0 0.0 copy-start
  8.0 0.0 all-reduce.2.cloned.1.call-start
  8.8 0.2 copy-done
  8.9 0.7 dynamic-slice_bitcast_fusion
  9.6 0.0 all-reduce.2.cloned.1.call-update
  9.6 0.0 all-gather.3.cloned.1.call-start
  9.7 0.5 all-gather.3.cloned.1.call-update
  10.2 0.0 reduce-scatter.2.cloned.1.call-start
  10.2 1.1 copy.35
  11.3 1.1 copy.36
  12.4 0.0 copy-start.1
  12.5 1.1 reshape.115
  13.6 0.1 iota_compare_fusion
  13.7 0.0 copy-start.2
  13.7 2.3 fusion.47
  16.0 0.0 copy-done.1
  16.0 0.0 copy-done.2
  16.0 1.3 convolution_convert_fusion.2
  17.3 7.2 %convolution_convert_fusion = bf16[512,7168]{1,0:T(8,128)(2,1)} fusion(bf16[512,256]{0,1:T(8,128)(2,1)S(1)} %bitcast.75, bf16[1,256,7168]{2,1,0:T(8,128)(2,1)} %param.12), kind=kOutput, calls=%fused_computation.2 | convolution fusion | flops 1882718208 | bytes 11272192 | tf_op jit(solution)/shard_map/dot_general | solution.py:57
  24.5 0.0 reduce-scatter.2.cloned.1.call-update
  24.5 235.7 %all-reduce.2.cloned.1.call-done = bf16[8,7168]{1,0:T(8,128)(2,1)} async-done(((bf16[8,7168]{1,0:T(8,128)(2,1)}), bf16[8,7168]{1,0:T(8,128)(2,1)}) %all-reduce.2.cloned.1.call-update) | async-done | bytes 114704 | tf_op jit(solution)/shard_map/psum | solution.py:28
  260.2 0.0 copy-done.4
  260.2 1.7 bitcast_subtract_fusion
  262.0 6.2 %fusion.24 = bf16[512,256]{0,1:T(8,128)(2,1)S(1)} fusion(bf16[1,256,7168]{2,1,0:T(8,128)(2,1)} %param.12, bf16[1,512,7168]{2,1,0:T(8,128)(2,1)} %all-gather.3.cloned.1.call-done), kind=kOutput, calls=%fused_computation.20 | convolution fusion | flops 1879179264 | bytes 11272192 | tf_op jit(solution)/shard_map/dot_general | solution.py:63
  268.2 0.4 fusion.37
  268.6 3.3 %fusion.18 = bf16[2,512,128]{1,2,0:T(8,128)(2,1)S(1)} fusion(bf16[512,2,128]{0,2,1:T(8,128)(2,1)} %bitcast.85, f32[2,512,512]{1,2,0:T(8,128)S(1)} %fusion.37, f32[2,512,512]{1,2,0:T(8,128)} %get-tuple-element.17, f32[2,512]{1,0:T(2,128)S(1)} %get-tuple-element.16), kind=kOutput, calls=%fused_computation.18 | convolution fusion | flops 138020352 | bytes 4722688 | tf_op jit(solution)/shard_map/shlm,smhd->slhd/dot_general | solution.py:79
  271.9 0.8 copy.27
  272.8 3.1 %fusion.21 = bf16[2,512,128]{1,2,0:T(8,128)(2,1)S(1)} fusion(bf16[512,2,128]{0,2,1:T(8,128)(2,1)S(1)} %bitcast.81, f32[2,512,512]{1,2,0:T(8,128)S(1)} %fusion.37, f32[2,512,512]{1,2,0:T(8,128)} %get-tuple-element.17, f32[2,512]{1,0:T(2,128)S(1)} %get-tuple-element.16), kind=kOutput, calls=%fused_computation.19 | convolution fusion | flops 138020352 | bytes 4722688 | tf_op jit(solution)/shard_map/shlm,slhd->smhd/dot_general | solution.py:82
  275.9 0.8 copy.28
  276.7 2.4 convolution_convert_fusion.3
  279.1 0.8 copy.29
  279.9 7.0 %fusion.2 = bf16[1,256,7168]{2,1,0:T(8,128)(2,1)} fusion(bf16[512,256]{0,1:T(8,128)(2,1)S(1)} %bitcast.76, bf16[1,512,7168]{2,1,0:T(8,128)(2,1)} %all-gather.3.cloned.1.call-done), kind=kOutput, calls=%fused_computation.4 | convolution fusion | flops 1880883200 | bytes 11272192 | tf_op jit(solution)/shard_map/dot_general | solution.py:68
  (5 shorter events, 0.0 us)
Async XLA Ops:
  8.0 0.9 copy-start
  8.0 252.2 %all-reduce.2.cloned.1.call-start = ((), (), s32[]{:S(2)}) async-start(), calls=%async_computation.2 | async-start | bytes 229376 | tf_op jit(solution)/shard_map/psum | solution.py:28
  9.6 252.3 %all-gather.3.cloned.1.call-start = ((), (), s32[]{:S(2)}) async-start(), calls=%async_computation.3 | async-start | bytes 7798784 | tf_op jit(solution)/shard_map/all_gather | solution.py:62
  10.2 276.7 %reduce-scatter.2.cloned.1.call-start = ((), (), s32[]{:S(2)}) async-start(), calls=%async_computation.1 | async-start | bytes 7798784 | tf_op jit(solution)/shard_map/reduce_scatter | solution.py:56
  12.4 3.5 %copy-start.1 = (bf16[1,512,256]{1,2,0:T(8,128)(2,1)}, bf16[1,512,256]{1,2,0:T(8,128)(2,1)S(1)}, u32[]{:S(2)}) copy-start(bf16[1,512,256]{1,2,0:T(8,128)(2,1)S(1)} %copy.36) | copy-start | bytes 786436
  13.7 2.3 copy-start.2
  24.5 235.8 %copy-start.3 = (f32[2,8,7168]{2,1,0:T(8,128)S(1)}, f32[2,8,7168]{2,1,0:T(8,128)}, u32[]{:S(2)}) copy-start(f32[2,8,7168]{2,1,0:T(8,128)} %param.15) | copy-start | bytes 1376260
  24.5 235.8 %copy-start.4 = (f32[2,8,7168]{2,1,0:T(8,128)S(1)}, f32[2,8,7168]{2,1,0:T(8,128)}, u32[]{:S(2)}) copy-start(f32[2,8,7168]{2,1,0:T(8,128)} %param.16) | copy-start | bytes 1376260
Sparse Core Ops, SparseCore 0:
  12.2 247.9 all-reduce.1
Sparse Core Ops, SparseCore 1:
  12.8 86.0 all-gather.2
  103.8 130.9 reduce-scatter.1
where the time goes:
time: 295 us; the launch traced here: 294 us
  waiting for transfers between devices  236 us (80%)
  matrix products  33.2 us (11%)
  between operations  16.3 us (6%)
  local copies, waits for them, and re-layouts  6.67 us (2%)
    psum x1, waiting for transfers between devices, outer_update(): summed = lax.psum(local_sel.astype(jnp.bfloat16), 'rep').astype(jnp.float32)  236 us
    dot_general x1, matrix products, inner_step(): jnp.dot(context_rows, weight_here, preferred_element_type=jnp.float32)  7.17 us
    dot_general x1, matrix products, inner_step(): lax.dot_general(context_rows, block_rows, (((0,), (0,)), ((), ())), prefe...  7 us
    dot_general x1, matrix products, inner_step(): lax.dot_general(block_rows, weight_here, (((1,), (1,)), ((), ())), prefer...  6.22 us
  transfers between devices with their start and end apart: 3, of which 1 were waited for; matrix products, arithmetic and copies ran while one was open for 14% of the time, Pallas kernels for 0%

commit v1 on v0

--- a/solution.py
+++ b/solution.py
@@ -25,7 +25,9 @@
     )
     outer_old = lax.dynamic_index_in_dim(global_params, chosen, 0, keepdims=False)
     moment_old = lax.dynamic_index_in_dim(momentum, chosen, 0, keepdims=False)
-    summed = lax.psum(local_sel.astype(jnp.bfloat16), "rep").astype(jnp.float32)
+    summed = jnp.sum(
+        jax.lax.all_gather(local_sel.astype(jnp.bfloat16), axis_name="rep"), axis=0
+    ).astype(jnp.float32)
     return nesterov(outer_old, moment_old, summed)
 
 

time: 295 us -> 333 us (1.13)
  the two profiles are of different devices: /device:TPU:128 before, /device:TPU:2 now
where the time goes in v1:
time: 333 us
  waiting for transfers between devices  275 us (83%)
  matrix products  34.2 us (10%)
  between operations  14.6 us (4%)
  local copies, waits for them, and re-layouts  6.68 us (2%)
    reduce_scatter x1, waiting for transfers between devices, inner_step(): lax.psum_scatter(jnp.dot(context_rows, weight_here, preferred_element_typ...  103 us
    all_gather x1, waiting for transfers between devices, inner_step(): block_rows = lax.all_gather(cotangent[0], 'tp', axis=0, tiled=True)  99.2 us
    all_gather x1, waiting for transfers between devices, outer_update(): jax.lax.all_gather(local_sel.astype(jnp.bfloat16), axis_name='rep')  72.1 us
    dot_general x1, matrix products, inner_step(): lax.dot_general(context_rows, block_rows, (((0,), (0,)), ((), ())), prefe...  7.61 us
    dot_general x1, matrix products, inner_step(): jnp.dot(context_rows, weight_here, preferred_element_type=jnp.float32)  7.17 us
  transfers between devices with their start and end apart: 3, of which 3 were waited for; matrix products, arithmetic and copies ran while one was open for 13% of the time, Pallas kernels for 0%

profile of v1, /device:TPU:2, one launch (start us, length us, event | category | flops | bytes accessed | tf_op | source)
XLA Modules:
  0.0 333.0 jit_solution(16740651389502273049)
XLA Ops:
  7.2 0.0 copy-start
  7.2 0.0 all-gather.7.cloned.1.call-start
  7.9 0.2 copy-done
  8.1 0.7 constant_dynamic-slice_fusion
  8.8 0.0 all-gather.7.cloned.1.call-update
  8.8 0.0 all-gather.5.cloned.1.call-start
  8.8 0.7 all-gather.5.cloned.1.call-update
  9.5 0.0 reduce-scatter.2.cloned.1.call-start
  9.6 1.1 copy.49
  10.7 1.1 copy.50
  11.8 0.0 copy-start.1
  11.8 1.1 reshape.116
  12.9 0.1 iota_compare_fusion
  13.0 2.3 fusion.47
  15.3 1.3 convolution_convert_fusion.2
  16.6 7.2 %convolution_convert_fusion = bf16[512,7168]{1,0:T(8,128)(2,1)} fusion(bf16[512,256]{0,1:T(8,128)(2,1)S(1)} %bitcast.73, bf16[1,256,7168]{2,1,0:T(8,128)(2,1)} %param.12), kind=kOutput, calls=%fused_computation.2 | convolution fusion | flops 1882718208 | bytes 11272192 | tf_op jit(solution)/shard_map/dot_general | solution.py:59
  23.8 0.0 reduce-scatter.2.cloned.1.call-update
  23.8 0.0 copy-start.4
  23.9 72.1 %all-gather.7.cloned.1.call-done = bf16[16,1,8,7168]{3,2,1,0:T(8,128)(2,1)} async-done(((bf16[1,1,8,7168]{3,2,1,0:T(8,128)(2,1)}), bf16[16,1,8,7168]{3,2,1,0:T(8,128)(2,1)}) %all-gather.7.cloned.1.call-update) | async-done | bytes 1835024 | tf_op jit(solution)/shard_map/all_gather | solution.py:29
  96.0 1.8 reduce_sum.32
  97.8 0.8 bitcast_subtract_fusion
  98.6 99.2 %all-gather.5.cloned.1.call-done = bf16[1,512,7168]{2,1,0:T(8,128)(2,1)} async-done(((bf16[1,32,7168]{2,1,0:T(8,128)(2,1)}), bf16[1,512,7168]{2,1,0:T(8,128)(2,1)}) %all-gather.5.cloned.1.call-update) | async-done | bytes 7340048 | tf_op jit(solution)/shard_map/all_gather | solution.py:64
  197.9 6.2 %fusion.24 = bf16[512,256]{0,1:T(8,128)(2,1)S(1)} fusion(bf16[1,256,7168]{2,1,0:T(8,128)(2,1)} %param.12, bf16[1,512,7168]{2,1,0:T(8,128)(2,1)} %all-gather.5.cloned.1.call-done), kind=kOutput, calls=%fused_computation.20 | convolution fusion | flops 1879179264 | bytes 11272192 | tf_op jit(solution)/shard_map/dot_general | solution.py:65
  204.1 0.4 fusion.37
  204.5 3.3 fusion.18
  207.8 0.8 copy.41
  208.7 3.4 %fusion.21 = bf16[2,512,128]{1,2,0:T(8,128)(2,1)S(1)} fusion(bf16[512,2,128]{0,2,1:T(8,128)(2,1)S(1)} %bitcast.79, f32[2,512,512]{1,2,0:T(8,128)S(1)} %fusion.37, f32[2,512,512]{1,2,0:T(8,128)} %get-tuple-element.24, f32[2,512]{1,0:T(2,128)S(1)} %get-tuple-element.23), kind=kOutput, calls=%fused_computation.19 | convolution fusion | flops 138020352 | bytes 4722688 | tf_op jit(solution)/shard_map/shlm,slhd->smhd/dot_general | solution.py:84
  212.1 0.8 copy.42
  212.9 2.4 convolution_convert_fusion.3
  215.3 0.8 copy.43
  216.2 7.6 %fusion.2 = bf16[1,256,7168]{2,1,0:T(8,128)(2,1)} fusion(bf16[512,256]{0,1:T(8,128)(2,1)S(1)} %bitcast.74, bf16[1,512,7168]{2,1,0:T(8,128)(2,1)} %all-gather.5.cloned.1.call-done), kind=kOutput, calls=%fused_computation.4 | convolution fusion | flops 1880883200 | bytes 11272192 | tf_op jit(solution)/shard_map/dot_general | solution.py:70
  223.8 102.6 %reduce-scatter.2.cloned.1.call-done = bf16[32,7168]{1,0:T(8,128)(2,1)} async-done(((bf16[512,7168]{1,0:T(8,128)(2,1)}), bf16[32,7168]{1,0:T(8,128)(2,1)}) %reduce-scatter.2.cloned.1.call-update) | async-done | bytes 458768 | tf_op jit(solution)/shard_map/reduce_scatter | solution.py:58
  (6 shorter events, 0.0 us)
Async XLA Ops:
  7.2 0.9 copy-start
  7.2 88.8 %all-gather.7.cloned.1.call-start = ((), (), s32[]{:S(2)}) async-start(), calls=%async_computation.3 | async-start | bytes 1949696 | tf_op jit(solution)/shard_map/all_gather | solution.py:29
  8.8 189.1 %all-gather.5.cloned.1.call-start = ((), (), s32[]{:S(2)}) async-start(), calls=%async_computation.2 | async-start | bytes 7798784 | tf_op jit(solution)/shard_map/all_gather | solution.py:64
  9.5 316.9 %reduce-scatter.2.cloned.1.call-start = ((), (), s32[]{:S(2)}) async-start(), calls=%async_computation.1 | async-start | bytes 7798784 | tf_op jit(solution)/shard_map/reduce_scatter | solution.py:58
  11.8 3.5 %copy-start.1 = (bf16[1,512,256]{1,2,0:T(8,128)(2,1)}, bf16[1,512,256]{1,2,0:T(8,128)(2,1)S(1)}, u32[]{:S(2)}) copy-start(bf16[1,512,256]{1,2,0:T(8,128)(2,1)S(1)} %copy.50) | copy-start | bytes 786436
  13.0 2.3 copy-start.2
  23.8 73.9 %copy-start.3 = (f32[2,8,7168]{2,1,0:T(8,128)S(1)}, f32[2,8,7168]{2,1,0:T(8,128)}, u32[]{:S(2)}) copy-start(f32[2,8,7168]{2,1,0:T(8,128)} %param.15) | copy-start | bytes 1376260
  23.8 73.9 %copy-start.4 = (f32[2,8,7168]{2,1,0:T(8,128)S(1)}, f32[2,8,7168]{2,1,0:T(8,128)}, u32[]{:S(2)}) copy-start(f32[2,8,7168]{2,1,0:T(8,128)} %param.16) | copy-start | bytes 1376260
Sparse Core Ops, SparseCore 0:
  10.4 85.5 all-gather.6
  98.7 99.1 all-gather.4
  202.9 123.4 reduce-scatter.1
